TPU v7x, 32 devices: a whole 2x2x4 slice. The times are simulated.
32 devices in a mesh: group: 2 (over y), sta: 4 (over z), win: 2 (over x), freq: 2 (over core).
Axes of the slice: x: 2, y: 2, z: 4, core: 2. Of those that a mesh axis runs over, the one named last changes fastest.
Arguments:
- records: float32 [1024, 4, 3600], P(('group', 'sta'), 'win', 'freq'), parts along dimension 0, may hold values from -6 to 6
- valid_counts: int32 [8], P(('group', 'sta')), parts along dimension 0, may hold values from 64 to 128, as said below
- pair_blocks: int32 [8, 2], P('group'), parts along dimension 0, may hold values from 0 to 3, as said below
Outputs:
- pair_spectra: bfloat16 [8, 2, 256, 2, 128, 128], P(('group', 'sta'), 'freq', 'win'), parts along dimension 0
There are 2 independent parts, one for each index of `group`. A program takes and returns all parts, laid end to end along the dimension named above; each array names one. Nothing has to cross between parts.
Inputs may be any that keep to these rules, and one draw needn't show every extreme that they name: The stations of block i at positions below valid_counts[i] are live, the others are masked out. `pair_blocks`: slot k belongs to index k // 1 of sta and names two station blocks.
All inputs are finite; a program needn't handle non-finite values.
Results may differ from a plain program's by a relative error of at most 0.001.
Values may be sent and summed in bfloat16 or wider, within the bound.
A program may use at most 64 MiB of HBM per device.

v0:
```python
import math
import jax
import jax.numpy as jnp
from jax import lax
from jax.sharding import PartitionSpec as P

SAMPLES = 3600
BINS = 512
HALF_WIDTH = 10
TWO_PI = 2.0 * math.pi
AMP_FLOOR = 0.1
PRECISE = lax.Precision.HIGHEST


def padded_2(value, sides, width):
    for axis, dim in sides:
        peers, length = (lax.axis_size(axis), value.shape[dim])
        up = [(i, (i + 1) % peers) for i in range(peers - 1)]
        down = [(j, i) for i, j in up]
        last = lax.slice_in_dim(value, length - width, length, axis=dim)
        first = lax.slice_in_dim(value, 0, width, axis=dim)
        before = lax.ppermute(last, axis, up)
        after = lax.ppermute(first, axis, down)
        value = jnp.concatenate([before, value, after], axis=dim)
    return value


def taper_of(sample_index, length_all):
    edge_len = length_all // 20
    position = jnp.minimum(sample_index, length_all - 1 - sample_index)
    ramped = 0.5 * (1.0 - jnp.cos(math.pi * (position.astype(jnp.float32) + 0.5) / edge_len))
    return jnp.where(position < edge_len, ramped, 1.0)


def dft_tables(bin_start, amount, sample_count, length_all):
    bin_index = bin_start + 1 + lax.broadcasted_iota(jnp.int32, (amount, sample_count), 0)
    sample_index = lax.broadcasted_iota(jnp.int32, (amount, sample_count), 1)
    angles = (bin_index * sample_index % length_all).astype(jnp.float32) * (TWO_PI / length_all)
    weight = taper_of(sample_index, length_all) / math.sqrt(length_all)
    return (jnp.cos(angles) * weight, -jnp.sin(angles) * weight)


def cross_pair(left_block, right_block):
    left_real = left_block[:, :, 0]
    left_imag = left_block[:, :, 1]
    stacked = jnp.stack(
        (jnp.stack((left_real, left_imag), 2), jnp.stack((left_imag, -left_real), 2)), 1
    )
    factor = 1.0 / math.sqrt(left_block.shape[1])
    return jnp.einsum("fpwqa,fwqb->fpab", stacked, right_block, precision=PRECISE) * factor


def local(records, valid_counts, pair_blocks):
    block_size = records.shape[0]
    band_bins = BINS // lax.axis_size("freq")
    first_bin = lax.axis_index("freq") * band_bins
    portion = lax.all_gather(records, "freq", axis=2, tiled=True)
    cos_table, sin_table = dft_tables(first_bin, band_bins, portion.shape[2], SAMPLES)
    real_part = jnp.einsum("kn,swn->kws", cos_table, portion, precision=PRECISE)
    imag_part = jnp.einsum("kn,swn->kws", sin_table, portion, precision=PRECISE)
    spectrum = jnp.stack((real_part, imag_part), 2)
    live_mask = (lax.broadcasted_iota(jnp.int32, (block_size,), 0) < valid_counts[0]).astype(
        jnp.float32
    )
    spectrum = spectrum * live_mask
    magnitude = jnp.sqrt(
        spectrum[:, :, 0] * spectrum[:, :, 0] + spectrum[:, :, 1] * spectrum[:, :, 1]
    )
    padded = padded_2(magnitude, (("freq", 0),), HALF_WIDTH)
    row_index = lax.broadcasted_iota(jnp.int32, (band_bins, band_bins + 2 * HALF_WIDTH), 0)
    col_index = lax.broadcasted_iota(jnp.int32, (band_bins, band_bins + 2 * HALF_WIDTH), 1)
    box_matrix = ((col_index - row_index >= 0) & (col_index - row_index <= 2 * HALF_WIDTH)).astype(
        jnp.float32
    )
    summed = jnp.einsum("ij,jws->iws", box_matrix, padded, precision=PRECISE)
    global_bin = first_bin + lax.broadcasted_iota(jnp.int32, (band_bins,), 0)
    counted = (
        jnp.minimum(global_bin + HALF_WIDTH, BINS - 1) - jnp.maximum(global_bin - HALF_WIDTH, 0) + 1
    ).astype(jnp.float32)
    smooth = summed / counted[:, None, None]
    whitened = spectrum / jnp.maximum(smooth, AMP_FLOOR)[:, :, None, :]
    sta_count = lax.axis_size("sta")
    slots = pair_blocks.shape[0] // sta_count
    my_slots = lax.dynamic_slice_in_dim(pair_blocks, lax.axis_index("sta") * slots, slots, 0)
    held_block = lax.all_to_all(whitened, "win", split_axis=0, concat_axis=1, tiled=True)
    blank_pair = jnp.zeros((slots,) + held_block.shape, jnp.float32)
    carried = (blank_pair, blank_pair)
    portion = lax.all_gather(held_block[None], "sta", axis=0, tiled=True)
    amount = portion.shape[0]
    chosen = []
    for column in range(2):
        wanted = my_slots[:, column]
        inside = (wanted >= 0) & (wanted < amount)
        fetched = jnp.take(portion, jnp.clip(wanted, 0, amount - 1), axis=0)
        chosen.append(jnp.where(inside[:, None, None, None, None], fetched, carried[column]))
    left_blocks = chosen[0]
    right_blocks = chosen[1]
    mixed = jax.vmap(cross_pair)(left_blocks, right_blocks).astype(jnp.bfloat16)
    return mixed[:, None]


def solution(mesh):
    in_specs = (P(("group", "sta"), "win", "freq"), P(("group", "sta")), P("group", None))
    out_specs = P(("group", "sta"), "freq", "win", None, None, None)
    return jax.shard_map(local, mesh=mesh, in_specs=in_specs, out_specs=out_specs, check_vma=False)
```

profile of v0, /device:TPU:0, one launch (start us, length us, event | category | flops | bytes accessed | tf_op | source)
XLA Modules:
  0.0 175.7 jit_solution(15182454830260234039)
XLA Ops:
  6.5 0.0 copy-start
  6.5 0.0 all-gather.3.cloned.1.call-start
  6.5 0.7 all-gather.3.cloned.1.call-update
  7.3 0.0 all-gather.5.cloned.1.call-start
  8.0 0.1 subtract_multiply_fusion
  8.1 16.5 %all-gather.3.cloned.1.call-done = f32[128,2,3600]{0,2,1:T(8,128)} async-done(((f32[128,2,1800]{0,2,1:T(8,128)}), f32[128,2,3600]{0,2,1:T(8,128)}) %all-gather.3.cloned.1.call-update) | async-done | bytes 3686416 | tf_op jit(solution)/shard_map/all_gather | solution.py:57
  24.6 0.0 copy-start.1
  24.6 25.0 %fusion.37 = f32[256,2,1,128]{3,0,1,2:T(8,128)S(1)} fusion(f32[128,2,3600]{0,2,1:T(8,128)} %all-gather.3.cloned.1.call-done, f32[3600]{0:T(1024)S(1)} %subtract_multiply_fusion, s32[256]{0:T(256)S(1)} %iota_add_fusion, pred[3600]{0:T(1024)(128)(4,1)S(1)} %fusion.65), kind=kOutput, calls=%fused_computation.35 | convolution fusion | flops 2843136000 | bytes 3967568 | tf_op jit(solution)/shard_map/kn,swn->kws/dot_general | solution.py:60
  49.6 0.0 copy-done.1
  49.6 21.3 %fusion.34 = f32[256,2,1,128]{3,0,1,2:T(8,128)S(1)} fusion(f32[128,2,3600]{0,2,1:T(8,128)S(1)} %copy-done.1, f32[3600]{0:T(1024)S(1)} %subtract_multiply_fusion, s32[256]{0:T(256)S(1)} %iota_add_fusion, pred[3600]{0:T(1024)(128)(4,1)S(1)} %fusion.65), kind=kOutput, calls=%fused_computation.34 | convolution fusion | flops 2842214400 | bytes 3967568 | tf_op jit(solution)/shard_map/kn,swn->kws/dot_general | solution.py:59
  70.9 0.1 fusion.58
  71.1 2.1 %collective-permute-start = (f32[10,2,128]{2,0,1:T(8,128)S(1)}, f32[10,2,128]{2,0,1:T(8,128)S(1)}, u32[]{:S(2)}, u32[]{:S(2)}) collective-permute-start(f32[10,2,128]{2,0,1:T(8,128)S(1)} %get-tuple-element.21), channel_id=1, source_target_pairs={{0,1},{2,3},{4,5},{6,7},{8,9},{10,11},{12,13},{14,15},{16,17},{18,... | collective-permute-start | bytes 30728 | tf_op jit(solution)/shard_map/ppermute | solution.py:22
  73.2 1.3 collective-permute-start.1
  74.5 0.1 fusion.86
  74.6 0.0 collective-permute-done
  74.6 1.7 collective-permute-done.1
  76.3 0.5 fusion.40
  76.8 0.1 broadcast_divide_fusion
  76.8 0.4 copy.6
  77.3 11.3 %all_to_all.15 = f32[256,2,2,128]{3,1,2,0:T(2,128)S(1)} all-to-all(f32[256,2,2,128]{3,1,2,0:T(2,128)S(1)} %copy.6), channel_id=1, replica_groups=mesh['group'=2,'sta'=4,'win'=2,'freq'=2] {'win'}, dimensions={0} | all-to-all | bytes 1048576 | tf_op jit(solution)/shard_map/all_to_all | solution.py:85
  88.5 0.8 copy.7
  89.3 0.0 all-gather.5.cloned.1.call-update
  89.4 0.0 copy-done
  89.4 0.1 constant_dynamic-slice_fusion.2
  89.4 0.5 fusion.82
  93.5 42.0 %all-gather.5.cloned.1.call-done = f32[4,128,4,2,128]{4,1,3,2,0:T(8,128)} async-done(((f32[1,128,4,2,128]{4,1,3,2,0:T(8,128)}), f32[4,128,4,2,128]{4,1,3,2,0:T(8,128)}) %all-gather.5.cloned.1.call-update) | async-done | bytes 2097168 | tf_op jit(solution)/shard_map/all_gather | solution.py:88
  135.6 1.3 constant_dynamic-slice_fusion
  136.8 0.5 fusion.85
  137.3 0.5 fusion.45
  137.8 0.1 fusion.81
  137.9 0.1 maximum_bitcast_fusion.1
  138.0 30.8 %fusion.1 = bf16[1,1,128,2,128,128]{5,4,3,2,1,0:T(8,128)(2,1)} fusion(f32[1,128,4,2,128]{4,1,3,2,0:T(8,128)S(1)} %get-tuple-element.17, pred[]{:T(512)} %bitcast.23, pred[]{:T(512)} %bitcast.21, f32[1,128,1,4,2,128]{5,3,4,1,2,0:T(4,128)S(1)} %maximum_bitcast_fusion.1, f32[1,128,1,4,2,128]{5,3,4,1,2,0:T(4,128)S(1)} %fusion.85), kind=kOutput, calls=%fused_computation.3 | convolution fusion | flops 411566080 | bytes 9961474 | tf_op jit(solution)/shard_map/vmap(fpwqa,fwqb->fpab)/dot_general | solution.py:50
  (6 shorter events, 0.1 us)
Async XLA Ops:
  6.5 82.8 %copy-start = (s32[4,2]{0,1:T(2,128)S(1)}, s32[4,2]{0,1:T(2,128)}, u32[]{:S(2)}) copy-start(s32[4,2]{0,1:T(2,128)} %param.7) | copy-start | bytes 100
  6.5 18.0 %all-gather.3.cloned.1.call-start = ((), (), s32[]{:S(2)}) async-start(), calls=%async_computation.1 | async-start | bytes 5529600 | tf_op jit(solution)/shard_map/all_gather | solution.py:57
  7.3 128.3 %all-gather.5.cloned.1.call-start = ((), (), s32[]{:S(2)}) async-start(), calls=%async_computation.2 | async-start | bytes 2621440 | tf_op jit(solution)/shard_map/all_gather | solution.py:88
  24.6 25.0 %copy-start.1 = (f32[128,2,3600]{0,2,1:T(8,128)S(1)}, f32[128,2,3600]{0,2,1:T(8,128)}, u32[]{:S(2)}) copy-start(f32[128,2,3600]{0,2,1:T(8,128)} %all-gather.3.cloned.1.call-done) | copy-start | bytes 11059204
  71.1 3.5 %collective-permute-start = (f32[10,2,128]{2,0,1:T(8,128)S(1)}, f32[10,2,128]{2,0,1:T(8,128)S(1)}, u32[]{:S(2)}, u32[]{:S(2)}) collective-permute-start(f32[10,2,128]{2,0,1:T(8,128)S(1)} %get-tuple-element.21), channel_id=1, source_target_pairs={{0,1},{2,3},{4,5},{6,7},{8,9},{10,11},{12,13},{14,15},{16,17},{18,... | collective-permute-start | bytes 30728 | tf_op jit(solution)/shard_map/ppermute | solution.py:22
  73.2 3.1 %collective-permute-start.1 = (f32[10,2,128]{2,0,1:T(8,128)S(1)}, f32[10,2,128]{2,0,1:T(8,128)S(1)}, u32[]{:S(2)}, u32[]{:S(2)}) collective-permute-start(f32[10,2,128]{2,0,1:T(8,128)S(1)} %get-tuple-element.22), channel_id=1, source_target_pairs={{1,0},{3,2},{5,4},{7,6},{9,8},{11,10},{13,12},{15,14},{17,16},{19,... | collective-permute-start | bytes 30728 | tf_op jit(solution)/shard_map/ppermute | solution.py:23
Sparse Core Ops, SparseCore 0:
  8.9 15.6 all-gather.2
  89.5 46.0 all-gather.4
where the time goes:
time: 176 us
  matrix products  77.6 us (44%)
  waiting for transfers between devices  60.9 us (35%)
  between operations  17.8 us (10%)
  blocking collectives  11.3 us (6%)
  starting transfers between devices  3.45 us (2%)
  local copies, waits for them, and re-layouts  3.12 us (2%)
    all_gather x1, waiting for transfers between devices, local(): portion = lax.all_gather(held_block[None], 'sta', axis=0, tiled=True)  42 us
    dot_general x1, matrix products, cross_pair(): jnp.einsum('fpwqa,fwqb->fpab', stacked, right_block, precision=PRECISE)  30.8 us
    dot_general x1, matrix products, local(): imag_part = jnp.einsum('kn,swn->kws', sin_table, portion, precision=PRECISE)  25 us
    dot_general x1, matrix products, local(): real_part = jnp.einsum('kn,swn->kws', cos_table, portion, precision=PRECISE)  21.3 us
    all_gather x1, waiting for transfers between devices, local(): portion = lax.all_gather(records, 'freq', axis=2, tiled=True)  16.5 us
    all_to_all x1, blocking collectives, local(): lax.all_to_all(whitened, 'win', split_axis=0, concat_axis=1, tiled=True)  11.3 us
  transfers between devices with their start and end apart: 4, of which 3 were waited for; matrix products, arithmetic and copies ran while one was open for 0% of the time, Pallas kernels for 0%

commit v1 on v0

--- a/solution.py
+++ b/solution.py
@@ -51,6 +51,30 @@
 
 
 def local(records, valid_counts, pair_blocks):
+
+    def bring_the_bars(array_in, a_name, dim_no):
+        everything, frame_out, current_value = (
+            lax.axis_size(a_name),
+            lax.axis_index(a_name),
+            array_in.shape[dim_no],
+        )
+        rack = tuple(
+            (c * everything if tick == dim_no else c for tick, c in enumerate(array_in.shape))
+        )
+        field_out = lax.dynamic_update_slice_in_dim(
+            jnp.zeros(rack, array_in.dtype), array_in, frame_out * current_value, axis=dim_no
+        )
+        for u in range(1, everything):
+            array_in = lax.ppermute(
+                array_in,
+                a_name,
+                tuple(((tick, (tick + 1) % everything) for tick in range(everything))),
+            )
+            field_out = lax.dynamic_update_slice_in_dim(
+                field_out, array_in, (frame_out - u) % everything * current_value, axis=dim_no
+            )
+        return field_out
+
     block_size = records.shape[0]
     band_bins = BINS // lax.axis_size("freq")
     first_bin = lax.axis_index("freq") * band_bins
@@ -85,7 +109,7 @@
     held_block = lax.all_to_all(whitened, "win", split_axis=0, concat_axis=1, tiled=True)
     blank_pair = jnp.zeros((slots,) + held_block.shape, jnp.float32)
     carried = (blank_pair, blank_pair)
-    portion = lax.all_gather(held_block[None], "sta", axis=0, tiled=True)
+    portion = bring_the_bars(held_block[None], "sta", 0)
     amount = portion.shape[0]
     chosen = []
     for column in range(2):

time: 176 us -> 169 us (0.960)
  waiting for transfers between devices: 60.9 us -> 53.8 us
    all_gather x1 -> x0, waiting for transfers between devices: 42 us -> none  [local(): portion = lax.all_gather(held_block[None], 'sta', axis=0, tiled=True)]
    ppermute x0 -> x3, waiting for transfers between devices: none -> 34.9 us  [bring_the_bars(): lax.ppermute(array_in, a_name, tuple(((tick, (tick + 1) % everything) for...]
  transfers between devices with their start and end apart: 4 -> 6, of which waited for: 3 -> 5; matrix products, arithmetic and copies ran while one was open for 0% -> 1% of each run, Pallas kernels for 0% -> 0%
where the time goes in v1:
time: 169 us
  matrix products  77.8 us (46%)
  waiting for transfers between devices  53.8 us (32%)
  between operations  18.1 us (11%)
  blocking collectives  11.2 us (7%)
  starting transfers between devices  5.11 us (3%)
  local copies, waits for them, and re-layouts  1.78 us (1%)
    ppermute x3, waiting for transfers between devices, bring_the_bars(): lax.ppermute(array_in, a_name, tuple(((tick, (tick + 1) % everything) for...  34.9 us
    dot_general x1, matrix products, cross_pair(): jnp.einsum('fpwqa,fwqb->fpab', stacked, right_block, precision=PRECISE)  31 us
    dot_general x1, matrix products, local(): imag_part = jnp.einsum('kn,swn->kws', sin_table, portion, precision=PRECISE)  25 us
    dot_general x1, matrix products, local(): real_part = jnp.einsum('kn,swn->kws', cos_table, portion, precision=PRECISE)  21.3 us
    all_gather x1, waiting for transfers between devices, local(): portion = lax.all_gather(records, 'freq', axis=2, tiled=True)  16.5 us
    all_to_all x1, blocking collectives, local(): lax.all_to_all(whitened, 'win', split_axis=0, concat_axis=1, tiled=True)  11.2 us
  transfers between devices with their start and end apart: 6, of which 5 were waited for; matrix products, arithmetic and copies ran while one was open for 1% of the time, Pallas kernels for 0%

profile of v1, /device:TPU:0, one launch (start us, length us, event | category | flops | bytes accessed | tf_op | source)
XLA Modules:
  0.0 168.7 jit_solution(11501678260353202749)
XLA Ops:
  6.5 0.0 copy-start
  6.5 0.0 all-gather.2.cloned.1.call-start
  6.5 0.7 all-gather.2.cloned.1.call-update
  8.0 0.1 subtract_multiply_fusion
  8.0 16.5 %all-gather.2.cloned.1.call-done = f32[128,2,3600]{0,2,1:T(8,128)} async-done(((f32[128,2,1800]{0,2,1:T(8,128)}), f32[128,2,3600]{0,2,1:T(8,128)}) %all-gather.2.cloned.1.call-update) | async-done | bytes 3686416 | tf_op jit(solution)/shard_map/all_gather | solution.py:81
  24.6 0.0 copy-start.1
  24.6 25.0 %fusion.37 = f32[256,2,1,128]{3,0,1,2:T(8,128)S(1)} fusion(f32[128,2,3600]{0,2,1:T(8,128)} %all-gather.2.cloned.1.call-done, f32[3600]{0:T(1024)S(1)} %subtract_multiply_fusion, s32[256]{0:T(256)S(1)} %iota_add_fusion, pred[3600]{0:T(1024)(128)(4,1)S(1)} %fusion.63), kind=kOutput, calls=%fused_computation.35 | convolution fusion | flops 2843136000 | bytes 3967568 | tf_op jit(solution)/shard_map/kn,swn->kws/dot_general | solution.py:84
  49.6 0.0 copy-done.1
  49.6 21.3 %fusion.34 = f32[256,2,1,128]{3,0,1,2:T(8,128)S(1)} fusion(f32[128,2,3600]{0,2,1:T(8,128)S(1)} %copy-done.1, f32[3600]{0:T(1024)S(1)} %subtract_multiply_fusion, s32[256]{0:T(256)S(1)} %iota_add_fusion, pred[3600]{0:T(1024)(128)(4,1)S(1)} %fusion.63), kind=kOutput, calls=%fused_computation.34 | convolution fusion | flops 2842214400 | bytes 3967568 | tf_op jit(solution)/shard_map/kn,swn->kws/dot_general | solution.py:83
  71.0 0.1 fusion.56
  71.1 2.1 %collective-permute-start = (f32[10,2,128]{2,0,1:T(8,128)S(1)}, f32[10,2,128]{2,0,1:T(8,128)S(1)}, u32[]{:S(2)}, u32[]{:S(2)}) collective-permute-start(f32[10,2,128]{2,0,1:T(8,128)S(1)} %get-tuple-element.19), channel_id=1, source_target_pairs={{0,1},{2,3},{4,5},{6,7},{8,9},{10,11},{12,13},{14,15},{16,17},{18,... | collective-permute-start | bytes 30728 | tf_op jit(solution)/shard_map/ppermute | solution.py:22
  73.2 1.3 collective-permute-start.1
  74.5 0.1 fusion.85
  74.6 0.0 collective-permute-done
  74.6 1.7 collective-permute-done.1
  76.3 0.5 fusion.40
  76.8 0.1 broadcast_divide_fusion
  76.8 0.4 copy.6
  77.3 11.2 %all_to_all.15 = f32[256,2,2,128]{3,1,2,0:T(2,128)S(1)} all-to-all(f32[256,2,2,128]{3,1,2,0:T(2,128)S(1)} %copy.6), channel_id=1, replica_groups=mesh['group'=2,'sta'=4,'win'=2,'freq'=2] {'win'}, dimensions={0} | all-to-all | bytes 1048576 | tf_op jit(solution)/shard_map/all_to_all | solution.py:109
  88.4 0.2 copy.7
  88.6 1.7 %collective-permute-start.2 = (f32[1,128,4,2,128]{4,2,3,1,0:T(4,128)S(1)}, f32[1,128,4,2,128]{4,2,3,1,0:T(4,128)S(1)}, u32[]{:S(2)}, u32[]{:S(2)}) collective-permute-start(f32[1,128,4,2,128]{4,2,3,1,0:T(4,128)S(1)} %bitcast.66), channel_id=1, source_target_pairs={{0,4},{4,8},{8,12},{12,0},{1,5},{5,9},{9,13},{13,1},{2,6},{6,10},{... | collective-permute-start | bytes 1572872 | tf_op jit(solution)/shard_map/ppermute | solution.py:68
  90.3 13.1 %collective-permute-done.2 = f32[1,128,4,2,128]{4,2,3,1,0:T(4,128)S(1)} collective-permute-done((f32[1,128,4,2,128]{4,2,3,1,0:T(4,128)S(1)}, f32[1,128,4,2,128]{4,2,3,1,0:T(4,128)S(1)}, u32[]{:S(2)}, u32[]{:S(2)}) %collective-permute-start.2) | collective-permute-done | bytes 524320 | tf_op jit(solution)/shard_map/ppermute | solution.py:68
  103.4 0.0 collective-permute-start.3
  103.5 13.8 %collective-permute-done.3 = f32[1,128,4,2,128]{4,2,3,1,0:T(4,128)S(1)} collective-permute-done((f32[1,128,4,2,128]{4,2,3,1,0:T(4,128)S(1)}, f32[1,128,4,2,128]{4,2,3,1,0:T(4,128)S(1)}, u32[]{:S(2)}, u32[]{:S(2)}) %collective-permute-start.3) | collective-permute-done | bytes 524320 | tf_op jit(solution)/shard_map/ppermute | solution.py:68
  117.3 0.0 collective-permute-start.4
  117.3 0.0 copy-done
  117.3 0.1 constant_dynamic-slice_fusion
  117.4 0.5 fusion.81
  121.8 0.3 broadcast_in_dim.47
  122.1 0.1 constant_dynamic-update-slice_fusion.3
  122.2 0.1 constant_dynamic-update-slice_fusion.2
  122.2 0.1 constant_dynamic-update-slice_fusion.1
  122.3 7.9 %collective-permute-done.4 = f32[1,128,4,2,128]{4,2,3,1,0:T(4,128)S(1)} collective-permute-done((f32[1,128,4,2,128]{4,2,3,1,0:T(4,128)S(1)}, f32[1,128,4,2,128]{4,2,3,1,0:T(4,128)S(1)}, u32[]{:S(2)}, u32[]{:S(2)}) %collective-permute-start.4) | collective-permute-done | bytes 524320 | tf_op jit(solution)/shard_map/ppermute | solution.py:68
  130.2 0.1 constant_dynamic-update-slice_fusion
  130.3 0.1 fusion.84
  130.4 0.1 select_select_fusion.2
  130.6 0.1 fusion.80
  130.7 0.1 maximum_bitcast_fusion.1
  130.8 31.0 %fusion.1 = bf16[1,1,128,2,128,128]{5,4,3,2,1,0:T(8,128)(2,1)} fusion(f32[4,128,4,2,128]{4,2,3,1,0:T(4,128)S(1)} %constant_dynamic-update-slice_fusion, s32[]{:T(128)} %bitcast.25, pred[]{:T(512)} %bitcast.24, pred[]{:T(512)} %bitcast.22, f32[1,128,1,4,2,128]{5,3,4,1,2,0:T(4,128)S(1)} %maximum_bitcast_fusion.1, f32[1,128,1,4,2,128]{5,3,4,1,2,0:T(4,128)S(1)} %fusion.84), kind=kOutput, calls=%fused_computation.3 | convolution fusion | flops 411566080 | bytes 9961478 | tf_op jit(solution)/shard_map/vmap(fpwqa,fwqb->fpab)/dot_general | solution.py:50
  (6 shorter events, 0.1 us)
Async XLA Ops:
  6.5 110.8 %copy-start = (s32[4,2]{0,1:T(2,128)S(1)}, s32[4,2]{0,1:T(2,128)}, u32[]{:S(2)}) copy-start(s32[4,2]{0,1:T(2,128)} %param.7) | copy-start | bytes 100
  6.5 18.0 %all-gather.2.cloned.1.call-start = ((), (), s32[]{:S(2)}) async-start(), calls=%async_computation.1 | async-start | bytes 5529600 | tf_op jit(solution)/shard_map/all_gather | solution.py:81
  24.6 25.0 %copy-start.1 = (f32[128,2,3600]{0,2,1:T(8,128)S(1)}, f32[128,2,3600]{0,2,1:T(8,128)}, u32[]{:S(2)}) copy-start(f32[128,2,3600]{0,2,1:T(8,128)} %all-gather.2.cloned.1.call-done) | copy-start | bytes 11059204
  71.1 3.5 %collective-permute-start = (f32[10,2,128]{2,0,1:T(8,128)S(1)}, f32[10,2,128]{2,0,1:T(8,128)S(1)}, u32[]{:S(2)}, u32[]{:S(2)}) collective-permute-start(f32[10,2,128]{2,0,1:T(8,128)S(1)} %get-tuple-element.19), channel_id=1, source_target_pairs={{0,1},{2,3},{4,5},{6,7},{8,9},{10,11},{12,13},{14,15},{16,17},{18,... | collective-permute-start | bytes 30728 | tf_op jit(solution)/shard_map/ppermute | solution.py:22
  73.2 3.1 %collective-permute-start.1 = (f32[10,2,128]{2,0,1:T(8,128)S(1)}, f32[10,2,128]{2,0,1:T(8,128)S(1)}, u32[]{:S(2)}, u32[]{:S(2)}) collective-permute-start(f32[10,2,128]{2,0,1:T(8,128)S(1)} %get-tuple-element.20), channel_id=1, source_target_pairs={{1,0},{3,2},{5,4},{7,6},{9,8},{11,10},{13,12},{15,14},{17,16},{19,... | collective-permute-start | bytes 30728 | tf_op jit(solution)/shard_map/ppermute | solution.py:23
  88.6 14.8 %collective-permute-start.2 = (f32[1,128,4,2,128]{4,2,3,1,0:T(4,128)S(1)}, f32[1,128,4,2,128]{4,2,3,1,0:T(4,128)S(1)}, u32[]{:S(2)}, u32[]{:S(2)}) collective-permute-start(f32[1,128,4,2,128]{4,2,3,1,0:T(4,128)S(1)} %bitcast.66), channel_id=1, source_target_pairs={{0,4},{4,8},{8,12},{12,0},{1,5},{5,9},{9,13},{13,1},{2,6},{6,10},{... | collective-permute-start | bytes 1572872 | tf_op jit(solution)/shard_map/ppermute | solution.py:68
  103.4 13.8 %collective-permute-start.3 = (f32[1,128,4,2,128]{4,2,3,1,0:T(4,128)S(1)}, f32[1,128,4,2,128]{4,2,3,1,0:T(4,128)S(1)}, u32[]{:S(2)}, u32[]{:S(2)}) collective-permute-start(f32[1,128,4,2,128]{4,2,3,1,0:T(4,128)S(1)} %collective-permute-done.2), channel_id=1, source_target_pairs={{0,4},{4,8},{8,12},{12,0},{1,5},{5,9},{9,13},{13,1},{2,6},{6,10},{... | collective-permute-start | bytes 1572872 | tf_op jit(solution)/shard_map/ppermute | solution.py:68
  117.3 12.9 %collective-permute-start.4 = (f32[1,128,4,2,128]{4,2,3,1,0:T(4,128)S(1)}, f32[1,128,4,2,128]{4,2,3,1,0:T(4,128)S(1)}, u32[]{:S(2)}, u32[]{:S(2)}) collective-permute-start(f32[1,128,4,2,128]{4,2,3,1,0:T(4,128)S(1)} %collective-permute-done.3), channel_id=1, source_target_pairs={{0,4},{4,8},{8,12},{12,0},{1,5},{5,9},{9,13},{13,1},{2,6},{6,10},{... | collective-permute-start | bytes 1572872 | tf_op jit(solution)/shard_map/ppermute | solution.py:68
Sparse Core Ops, SparseCore 0:
  8.9 15.6 all-gather.1
